TPU v7x, 768 devices: a whole 4x8x12 slice. The times are simulated.
768 devices in a mesh: blk: 16 (over y, core), cur: 48 (over x, z).
Axes of the slice: x: 4, y: 8, z: 12, core: 2. Of those that a mesh axis runs over, the one named last changes fastest.
Arguments:
- state: float32 [24576, 10240], P(('blk', 'cur')), may hold values from -6 to 6
- neighbour: int32 [24576, 4], P(('blk', 'cur')), may hold values from 0 to 24575, as said below
- neighbour_edge: int32 [24576, 4], P(('blk', 'cur')), may hold values from 0 to 3
- owner: int32 [24576, 1], P(('blk', 'cur')), may hold values from 0 to 47; in each aligned block of 32 rows (0 to 31, 32 to 63, ...) at most 2 rows name the same one
- surface: float32 [768, 384], P(('blk', 'cur')), may hold values from 0.5 to 1.5
- k_water: float32 [128, 128], replicated, may hold values from 0.002 to 0.2
- k_tracer: float32 [128, 128], replicated, may hold values from 0.002 to 0.2
Outputs:
- new_state: float32 [24576, 10240], P(('blk', 'cur'))
Inputs may be any that keep to these rules, and one draw needn't show every extreme that they name: neighbour[e, k] = (e + s) mod 24576 with 1 <= |s| <= 32; for every element e with e % 32 == 0, edge 0 has s = -32, and for e % 32 == 31, edge 2 has s = 32. Among the elements of one device, no owner is named more than 2 times, a bound that some block reaches.
All inputs are finite; a program needn't handle non-finite values.
Results may differ from a plain program's by a relative error of at most 0.0003.
Values sent between devices are 32-bit elements; how exact they have to be, the bound alone decides.
A program may use at most 64 MiB of HBM per device.

v0:
```python
import jax
import jax.numpy as jnp
import numpy as np
from jax import lax
from jax.sharding import PartitionSpec as P

HIGHEST = lax.Precision.HIGHEST


def extended(value, sides, width):
    edges = {}
    for axis, dim in sides:
        count, length = (lax.axis_size(axis), value.shape[dim])
        up = [(i, (i + 1) % count) for i in range(count)]
        last = lax.slice_in_dim(value, length - width, length, axis=dim)
        first = lax.slice_in_dim(value, 0, width, axis=dim)
        edges[dim] = (
            lax.ppermute(last, axis, up),
            lax.ppermute(first, axis, [(b, a) for a, b in up]),
        )
    done = []
    for _, dim in sides:
        low, high = edges[dim]
        around = [(width, width) if d in done else (0, 0) for d in range(value.ndim)]
        value = jnp.concatenate([jnp.pad(low, around), value, jnp.pad(high, around)], axis=dim)
        done.append(dim)
    return value


def gll_matrix():
    gll_nodes = np.array([-1.0, -1.0 / np.sqrt(5.0), 1.0 / np.sqrt(5.0), 1.0])
    weights = np.array(
        [
            1.0
            / np.prod(
                [
                    gll_nodes[col_at] - gll_nodes[other_at]
                    for other_at in range(4)
                    if other_at != col_at
                ]
            )
            for col_at in range(4)
        ]
    )
    matrix = np.zeros((4, 4))
    for row_at in range(4):
        for col_at in range(4):
            if row_at != col_at:
                matrix[row_at, col_at] = (
                    weights[col_at] / weights[row_at] / (gll_nodes[row_at] - gll_nodes[col_at])
                )
        matrix[row_at, row_at] = -np.sum(matrix[row_at])
    return matrix


def edge_table():
    return np.array([[0, 4, 8, 12], [12, 13, 14, 15], [15, 11, 7, 3], [3, 2, 1, 0]])


def boundary_points():
    return np.array([0, 1, 2, 3, 4, 7, 8, 11, 12, 13, 14, 15])


def boundary_edge_table():
    points = boundary_points()
    where_at = np.zeros(16, dtype=np.int64)
    where_at[points] = np.arange(12)
    return where_at[edge_table()]


def column_tables():
    quad_weights = np.array([1.0 / 6.0, 5.0 / 6.0, 5.0 / 6.0, 1.0 / 6.0])
    project = np.zeros((4, 16))
    inject = np.zeros((16, 4))
    for row_at in range(4):
        for col_at in range(4):
            column_id = 2 * (row_at // 2) + col_at // 2
            project[column_id, 4 * row_at + col_at] = quad_weights[row_at] * quad_weights[col_at]
            inject[4 * row_at + col_at, column_id] = 1.0
    return (project, inject)


def tendency(state3):
    count = state3.shape[0]
    points_grid = state3.reshape(count, 4, 4, state3.shape[2], state3.shape[3])
    derivative = jnp.asarray(gll_matrix(), jnp.float32)
    along_x = jnp.einsum("ia,eajvl->eijvl", derivative, points_grid, precision=HIGHEST)
    along_y = jnp.einsum("jb,eibvl->eijvl", derivative, points_grid, precision=HIGHEST)
    east_wind = points_grid[:, :, :, 0:1, :]
    north_wind = points_grid[:, :, :, 1:2, :]
    result = -0.5 * (east_wind * along_x + north_wind * along_y)
    return result.reshape(state3.shape)


def pick_neighbours(edges_all, index_rows, edge_id):
    flat = edges_all.reshape(edges_all.shape[0] * 4, 4, edges_all.shape[2], edges_all.shape[3])
    picked = jnp.take(flat, index_rows * 4 + edge_id, axis=0)
    return picked[:, :, ::-1]


def assemble(own_tend, picked):
    table = edge_table()
    onehot = (table[:, :, None] == np.arange(16)[None, None, :]).astype(np.float32)
    counts = 1.0 + onehot.sum(axis=(0, 1))
    gathered = jnp.einsum(
        "ekp,xekvl->xpvl", jnp.asarray(onehot, jnp.float32), picked, precision=HIGHEST
    )
    return (own_tend + gathered) / jnp.asarray(counts, jnp.float32)[None, :, None, None]


def to_columns(state3):
    project, inject = column_tables()
    thermo = state3[:, :, 2:5, :]
    return jnp.einsum("cp,epvl->ecvl", jnp.asarray(project, jnp.float32), thermo, precision=HIGHEST)


def physics(columns, surface_values, k_water, k_tracer):
    temper = columns[:, 0, :]
    water = jax.nn.softplus(columns[:, 1, :])
    tracer = jax.nn.softplus(columns[:, 2, :])
    depth = water[:, :, None] * k_water[None] + tracer[:, :, None] * k_tracer[None]
    path_in = jnp.cumsum(depth, axis=1)
    path_out = path_in - depth
    path_all = path_in[:, -1:, :]
    downward = jnp.mean(jnp.exp(-path_out) - jnp.exp(-path_in), axis=2)
    upward = jnp.mean(jnp.exp(path_in - path_all) - jnp.exp(path_out - path_all), axis=2)
    emitted = jnp.mean(1.0 - jnp.exp(-depth), axis=2)
    return (
        64.0 * downward + 2.0 * surface_values[:, None] * upward - 8.0 * jnp.tanh(temper) * emitted
    )


def physics_blocks(columns, surface_values, k_water, k_tracer):
    column_count = columns.shape[0]
    block_size = 128
    blocks = column_count // block_size
    col_blocks = columns.reshape(blocks, block_size, columns.shape[1], columns.shape[2])
    surf_blocks = surface_values.reshape(blocks, block_size)
    result = lax.map(
        lambda block_pair: physics(block_pair[0], block_pair[1], k_water, k_tracer),
        (col_blocks, surf_blocks),
    )
    return result.reshape(column_count, columns.shape[2])


def slot_ranks(owner_id):
    count = owner_id.shape[0]
    same_owner = owner_id[:, None] == owner_id[None, :]
    earlier = jnp.arange(count)[None, :] < jnp.arange(count)[:, None]
    return jnp.sum((same_owner & earlier).astype(jnp.int32), axis=1)


def update(state3, dss, heating):
    project, inject = column_tables()
    at_points = jnp.einsum(
        "pc,ecl->epl", jnp.asarray(inject, jnp.float32), heating, precision=HIGHEST
    )
    zeros_two = jnp.zeros((state3.shape[0], state3.shape[1], 2, state3.shape[3]), jnp.float32)
    physics_term = jnp.concatenate([zeros_two, at_points[:, :, None, :], zeros_two], axis=2)
    return state3 + 0.2 * (dss + physics_term)


def per_device(state, neighbour, neighbour_edge, owner, surface, k_water, k_tracer):
    elem_count = state.shape[0]
    levels = k_water.shape[0]
    cur_count = lax.axis_size("cur")
    device_count = lax.axis_size("blk") * cur_count
    my_index = lax.axis_index("blk") * cur_count + lax.axis_index("cur")
    total_elems = elem_count * device_count
    state3 = state.reshape(elem_count, 16, 5, levels)
    offset_base = my_index * elem_count - elem_count
    local_index = jnp.mod(neighbour - offset_base, total_elems)
    tendency_own = tendency(state3)
    rim_points = jnp.take(tendency_own, jnp.asarray(boundary_points(), jnp.int32), axis=1)
    rim_wide = extended(rim_points.reshape(elem_count, -1), ((("blk", "cur"), 0),), elem_count)
    rim_wide = rim_wide.reshape(3 * elem_count, 12, 5, levels)
    edges_wide = jnp.take(
        rim_wide, jnp.asarray(boundary_edge_table().reshape(-1), jnp.int32), axis=1
    )
    picked = pick_neighbours(edges_wide, local_index, neighbour_edge)
    dss = assemble(tendency_own, picked)
    columns = to_columns(state3).reshape(elem_count, 12 * levels)
    capacity = surface.shape[1] // (cur_count * 4)
    owner_id = owner[:, 0]
    slot_index = owner_id * capacity + slot_ranks(owner_id)
    select = (
        slot_index[:, None] == jnp.arange(cur_count * capacity, dtype=jnp.int32)[None, :]
    ).astype(jnp.float32)
    fetched = lax.all_to_all(
        surface.reshape(cur_count, capacity * 4), "cur", split_axis=0, concat_axis=0, tiled=True
    )
    surf_own = jnp.dot(select, fetched.reshape(cur_count * capacity, 4), precision=HIGHEST)
    heating = physics_blocks(
        columns.reshape(elem_count * 4, 3, levels), surf_own.reshape(-1), k_water, k_tracer
    )
    result = update(state3, dss, heating.reshape(elem_count, 4, levels))
    return result.reshape(elem_count, 16 * 5 * levels)


def solution(mesh):
    return jax.shard_map(
        per_device,
        mesh=mesh,
        in_specs=(
            P(("blk", "cur"), None),
            P(("blk", "cur"), None),
            P(("blk", "cur"), None),
            P(("blk", "cur"), None),
            P(("blk", "cur"), None),
            P(),
            P(),
        ),
        out_specs=P(("blk", "cur"), None),
        check_vma=False,
    )
```

profile of v0, /device:TPU:1, one launch (start us, length us, event | category | flops | bytes accessed | tf_op | source)
XLA Modules:
  0.0 97.6 jit_solution(13758927542508641136)
XLA Ops:
  0.0 1.9 %reshape_reshape.2 = f32[32,4,4,5,128]{4,3,2,1,0:T(8,128)S(1)} reshape(f32[32,10240]{1,0:T(8,128)} %param.14) | data formatting | bytes 2621440 | tf_op jit(solution)/shard_map/reshape;reshape | solution.py:85
  1.9 0.4 fusion.29
  2.5 2.3 %fusion.14 = f32[4,32,4,5,128]{4,0,3,2,1:T(4,128)S(1)} fusion(f32[4,4,1,1,1]{1,0,4,3,2:T(4,128)S(1)} %copy-done.9, f32[32,4,4,5,128]{4,3,2,1,0:T(8,128)S(1)} %reshape_reshape.2), kind=kOutput, calls=%fused_computation.26 | convolution fusion | flops 15728640 | bytes 2621504 | tf_op jit(solution)/shard_map/jb,eibvl->eijvl/dot_general | solution.py:88
  4.8 3.3 %fusion.8 = f32[32,4,4,5,128]{4,1,3,2,0:T(4,128)S(1)} fusion(f32[4,4,1,1,1]{1,0,4,3,2:T(4,128)S(1)} %copy-done.9, f32[4,32,4,5,128]{4,0,3,2,1:T(4,128)S(1)} %fusion.14, f32[32,4,4,5,128]{4,3,2,1,0:T(8,128)S(1)} %reshape_reshape.2, f32[32,4,4,128]{3,1,2,0:T(4,128)S(1)} %copy.97, f32[32,4,4,128]{3,1,2,0:T(4,128)S(1)} %copy.95), kind=kOutput, calls=%fused_computation.17 | convolution fusion | flops 17039360 | bytes 4456512 | tf_op jit(solution)/shard_map/ia,eajvl->eijvl/dot_general | solution.py:87
  8.2 0.4 copy.100
  8.6 0.2 copy-done.17
  8.8 0.6 gather_fusion
  9.5 1.8 %copy.102 = f32[32,12,5,128]{3,2,1,0:T(8,128)} copy(f32[32,12,5,128]{3,0,2,1:T(8,128)S(1)} %bitcast.75) | data formatting | bytes 1966080 | tf_op jit(solution)/shard_map/jit(_take)/gather | solution.py:174
  11.2 1.7 %gather.17 = f32[32,7680]{1,0:T(8,128)S(1)} reshape(f32[32,12,5,128]{3,2,1,0:T(8,128)} %copy.102) | data formatting | bytes 1966080 | tf_op jit(solution)/shard_map/jit(_take)/gather | solution.py:174
  13.0 4.8 %collective-permute-start = (f32[32,7680]{1,0:T(8,128)S(1)}, f32[32,7680]{1,0:T(8,128)}, u32[]{:S(2)}, u32[]{:S(2)}) collective-permute-start(f32[32,7680]{1,0:T(8,128)S(1)} %gather.17), channel_id=1, source_target_pairs={{0,1},{1,2},{2,3},{3,4},{4,5},{5,6},{6,7},{7,8},{8,9},{9,10},{10,1... | collective-permute-start | bytes 2949128 | tf_op jit(solution)/shard_map/ppermute | solution.py:18
  17.8 15.0 %collective-permute-start.1 = (f32[32,7680]{1,0:T(8,128)S(1)}, f32[32,7680]{1,0:T(8,128)}, u32[]{:S(2)}, u32[]{:S(2)}) collective-permute-start(f32[32,7680]{1,0:T(8,128)S(1)} %gather.17), channel_id=1, source_target_pairs={{1,0},{2,1},{3,2},{4,3},{5,4},{6,5},{7,6},{8,7},{9,8},{10,9},{11,1... | collective-permute-start | bytes 2949128 | tf_op jit(solution)/shard_map/ppermute | solution.py:19
  32.8 0.7 all_to_all.6
  33.5 4.6 %all-to-all-start = ((f32[48,1,8]{2,1,0:T(1,128)}), f32[48,1,8]{2,1,0:T(1,128)S(1)}, u32[]{:S(2)}, u32[]{:S(2)}) async-start(f32[48,1,8]{2,1,0:T(1,128)} %bitcast.28), calls=%async_computation | async-start | bytes 49152 | tf_op jit(solution)/shard_map/all_to_all | solution.py:189
  38.1 1.9 %reshape.123 = f32[32,16,5,128]{3,2,1,0:T(8,128)S(1)} reshape(f32[32,10240]{1,0:T(8,128)} %param.14) | data formatting | bytes 2621440 | tf_op jit(solution)/shard_map/reshape | solution.py:170
  40.1 0.3 slice.40
  40.4 0.5 convolution_bitcast_fusion.2
  41.1 0.1 copy.111
  41.2 0.1 copy.112
  41.3 8.5 %fusion.1 = f32[128,128,128]{2,0,1:T(8,128)} fusion(f32[128,128]{1,0:T(8,128)} %param.20, f32[128,128]{0,1:T(8,128)S(1)} %copy.112, f32[128,128]{1,0:T(8,128)} %param.19, f32[128,128]{0,1:T(8,128)S(1)} %copy.111), kind=kOutput, calls=%fused_computation.8 | output fusion | flops 272629760 | bytes 8650752 | tf_op jit(solution)/shard_map/while/body/eval_jaxpr/jit(cumsum)/reduce_window_sum | solution.py:122
  49.8 0.8 slice_bitcast_fusion
  50.7 15.1 %subtract_reduce_fusion.1 = (f32[128,128]{0,1:T(8,128)S(1)}, f32[128,128]{0,1:T(8,128)S(1)}, f32[128,128]{0,1:T(8,128)S(1)}) fusion(f32[128,128,128]{2,0,1:T(8,128)} %fusion.1, f32[128,128]{1,0:T(8,128)S(1)} %slice_bitcast_fusion, f32[128,128]{1,0:T(8,128)S(1)} %copy-done.7, f32[128,128]{0,1:T(8,128)S(1)} %copy.112, f32[128,128]{1,0:T(8,128)} %param.19, ...), kind=kLoop, calls=%fused_computation.4 | loop fusion | flops 31408128 | bytes 8912896 | tf_op jit(solution)/shard_map/while/body/eval_jaxpr/reduce_sum | solution.py:126
  65.8 0.2 convert_reduce_fusion
  66.1 0.1 copy.106
  66.1 0.1 reshape.145
  66.4 0.1 copy.117
  66.5 0.1 copy.114
  66.6 0.1 copy.101
  66.7 0.5 broadcast.124
  67.2 0.6 reduce.4
  68.0 0.2 convolution_multiply_fusion
  68.2 0.1 copy.116
  68.3 1.2 %convolution_bitcast_fusion.1 = f32[32,16,1,128]{3,1,0,2:T(8,128)} fusion(f32[16,4,1]{0,1,2:T(4,128)S(1)} %copy-done.10, f32[32,4,128]{2,1,0:T(4,128)S(1)} %bitcast.83, f32[32,4,128]{2,1,0:T(4,128)S(1)} %bitcast.85, f32[32,4,128]{2,1,0:T(4,128)S(1)} %bitcast.84, f32[32,4,128]{2,1,0:T(4,128)S(1)} %bitcast.86, f32[32,4]{1,0:T(8,128)S(1)} %copy.116), kind=kOutput, calls=%fused_computation.29 | convolution fusion | flops 3211264 | bytes 525056 | tf_op jit(solution)/shard_map/pc,ecl->epl/dot_general | solution.py:155
  69.4 1.7 %concatenate.11 = f32[32,12,5,128]{3,2,1,0:T(8,128)S(1)} reshape(f32[32,7680]{1,0:T(8,128)} %collective-permute-done) | data formatting | bytes 1966080 | tf_op jit(solution)/shard_map/concatenate | solution.py:25
  71.1 1.5 %copy.103 = f32[32,12,5,128]{3,0,2,1:T(8,128)} copy(f32[32,12,5,128]{3,2,1,0:T(8,128)S(1)} %concatenate.11) | data formatting | bytes 1966080 | tf_op jit(solution)/shard_map/concatenate | solution.py:25
  72.7 1.7 %concatenate.12 = f32[32,12,5,128]{3,2,1,0:T(8,128)S(1)} reshape(f32[32,7680]{1,0:T(8,128)} %collective-permute-done.1) | data formatting | bytes 1966080 | tf_op jit(solution)/shard_map/concatenate | solution.py:25
  74.4 0.6 copy.104
  75.0 0.6 copy-done.5
  75.6 1.4 %pad_maximum_fusion = f32[96,12,5,128]{3,0,2,1:T(8,128)S(1)} fusion(f32[32,12,5,128]{3,0,2,1:T(8,128)S(1)} %copy.104, f32[32,12,5,128]{3,0,2,1:T(8,128)} %bitcast.76, f32[32,12,5,128]{3,0,2,1:T(8,128)S(1)} %copy-done.5), kind=kLoop, calls=%fused_computation.13 | loop fusion | flops 1474560 | bytes 5898240 | tf_op jit(solution)/shard_map/concatenate | solution.py:25
  77.0 2.7 %gather_fusion.1 = f32[16,96,5,128]{3,1,2,0:T(8,128)} fusion(f32[96,12,5,128]{3,0,2,1:T(8,128)S(1)} %pad_maximum_fusion, s32[1024]{0:T(1024)S(1)} %pad_clamp_fusion.1), kind=kCustom, calls=%fused_computation.1 | custom fusion | bytes 7864384 | tf_op jit(solution)/shard_map/jit(_take)/gather | solution.py:177
  79.7 6.2 %copy.105 = f32[96,16,5,128]{3,1,0,2:T(8,128)} copy(f32[96,16,5,128]{3,0,2,1:T(8,128)} %bitcast.72) | data formatting | bytes 7864320 | tf_op jit(solution)/shard_map/jit(_take)/gather | solution.py:177
  85.9 3.7 %gather_fusion.2 = f32[128,4,5,128]{3,1,2,0:T(4,128)S(1)} fusion(f32[384,4,5,128]{3,1,0,2:T(4,128)} %bitcast.77, s32[1024]{0:T(1024)S(1)} %pad_clamp_fusion), kind=kCustom, calls=%fused_computation.2 | custom fusion | bytes 2621952 | tf_op jit(solution)/shard_map/jit(_take)/gather | solution.py:97
  89.6 0.1 copy.107
  89.7 0.4 broadcast_select_fusion
  90.2 1.1 %rev.3 = f32[32,4,4,5,128]{4,1,0,3,2:T(4,128)} reverse(f32[32,4,4,5,128]{4,1,0,3,2:T(4,128)S(1)} %broadcast_select_fusion), dimensions={2} | reverse | bytes 2621440 | tf_op jit(solution)/shard_map/rev | solution.py:98
  91.3 2.8 %fusion.12 = f32[32,5,128,16,1]{2,3,1,0,4:T(8,128)S(1)} fusion(f32[4,4,16,1,1]{2,0,4,3,1:T(4,128)S(1)} %copy-done.8, f32[32,4,4,5,128]{4,1,0,3,2:T(4,128)} %rev.3), kind=kOutput, calls=%fused_computation.24 | convolution fusion | flops 62914560 | bytes 2622464 | tf_op jit(solution)/shard_map/ekp,xekvl->xpvl/dot_general | solution.py:105
  94.2 1.1 %fusion.10 = f32[32,16,5,128]{3,1,0,2:T(8,128)S(1)} fusion(f32[32,16,2,128]{3,1,0,2:T(8,128)S(1)} %broadcast_in_dim.91, f32[32,16,1,128]{3,1,0,2:T(8,128)S(1)} %copy-done.6, f32[32,5,128,16,1]{2,3,1,0,4:T(8,128)S(1)} %fusion.12, f32[32,16,5,128]{3,2,1,0:T(8,128)S(1)} %copy-done.3, f32[32,16,5,128]{3,0,2,1:T(8,128)S(1)} %bitcast.74, f32[16]{0:T(128)S(1)} %copy-done.15), kind=kLoop, calls=%fused_computation.20 | loop fusion | flops 2293760 | bytes 6029376 | tf_op jit(solution)/shard_map/add | solution.py:160
  95.3 0.8 copy.119
  96.1 1.5 %reshape.126 = f32[32,10240]{1,0:T(8,128)} reshape(f32[32,16,5,128]{3,2,1,0:T(8,128)S(1)} %copy.119) | data formatting | bytes 2621440 | tf_op jit(solution)/shard_map/reshape | solution.py:197
  (54 shorter events, 0.6 us)
Async XLA Ops:
  0.0 2.5 %copy-start.9 = (f32[4,4,1,1,1]{1,0,4,3,2:T(4,128)S(1)}, f32[4,4,1,1,1]{1,0,4,3,2:T(4,128)}, u32[]{:S(2)}) copy-start(f32[4,4,1,1,1]{1,0,4,3,2:T(4,128)} %constant.163) | copy-start | bytes 196
  8.2 0.7 copy-start.17
  8.8 2.4 %copy-start = (f32[32,4,4,5,128]{4,0,3,2,1:T(8,128)}, f32[32,4,4,5,128]{4,0,3,2,1:T(8,128)S(1)}, u32[]{:S(2)}) copy-start(f32[32,4,4,5,128]{4,0,3,2,1:T(8,128)S(1)} %copy.100) | copy-start | bytes 3932164
  9.4 3.5 %copy-start.4 = (f32[12,32,5,128]{3,1,2,0:T(8,128)}, f32[12,32,5,128]{3,1,2,0:T(8,128)S(1)}, u32[]{:S(2)}) copy-start(f32[12,32,5,128]{3,1,2,0:T(8,128)S(1)} %gather_fusion) | copy-start | bytes 2949124
  9.5 23.3 %copy-start.14 = (f32[1,384]{1,0:T(1,128)S(1)}, f32[1,384]{1,0:T(1,128)}, u32[]{:S(2)}) copy-start(f32[1,384]{1,0:T(1,128)} %param.18) | copy-start | bytes 4612
  13.0 56.5 %collective-permute-start = (f32[32,7680]{1,0:T(8,128)S(1)}, f32[32,7680]{1,0:T(8,128)}, u32[]{:S(2)}, u32[]{:S(2)}) collective-permute-start(f32[32,7680]{1,0:T(8,128)S(1)} %gather.17), channel_id=1, source_target_pairs={{0,1},{1,2},{2,3},{3,4},{4,5},{5,6},{6,7},{7,8},{8,9},{9,10},{10,1... | collective-permute-start | bytes 2949128 | tf_op jit(solution)/shard_map/ppermute | solution.py:18
  17.8 54.9 %collective-permute-start.1 = (f32[32,7680]{1,0:T(8,128)S(1)}, f32[32,7680]{1,0:T(8,128)}, u32[]{:S(2)}, u32[]{:S(2)}) collective-permute-start(f32[32,7680]{1,0:T(8,128)S(1)} %gather.17), channel_id=1, source_target_pairs={{1,0},{2,1},{3,2},{4,3},{5,4},{6,5},{7,6},{8,7},{9,8},{10,9},{11,1... | collective-permute-start | bytes 2949128 | tf_op jit(solution)/shard_map/ppermute | solution.py:19
  33.5 33.2 %all-to-all-start = ((f32[48,1,8]{2,1,0:T(1,128)}), f32[48,1,8]{2,1,0:T(1,128)S(1)}, u32[]{:S(2)}, u32[]{:S(2)}) async-start(f32[48,1,8]{2,1,0:T(1,128)} %bitcast.28), calls=%async_computation | async-start | bytes 49152 | tf_op jit(solution)/shard_map/all_to_all | solution.py:189
  38.1 2.3 %copy-start.11 = (f32[4,16,1,1]{1,0,3,2:T(4,128)S(1)}, f32[4,16,1,1]{1,0,3,2:T(4,128)}, u32[]{:S(2)}) copy-start(f32[4,16,1,1]{1,0,3,2:T(4,128)} %constant.165) | copy-start | bytes 772
  40.1 9.7 %copy-start.2 = (f32[32,16,5,128]{3,2,1,0:T(8,128)}, f32[32,16,5,128]{3,2,1,0:T(8,128)S(1)}, u32[]{:S(2)}) copy-start(f32[32,16,5,128]{3,2,1,0:T(8,128)S(1)} %reshape.123) | copy-start | bytes 3932164
  41.3 9.4 %copy-start.7 = (f32[128,128]{1,0:T(8,128)S(1)}, f32[128,128]{1,0:T(8,128)}, u32[]{:S(2)}) copy-start(f32[128,128]{1,0:T(8,128)} %param.20) | copy-start | bytes 196612
  50.6 15.2 %copy-start.18 = (s32[32,1]{0,1:T(1,128)S(1)}, s32[32,1]{0,1:T(1,128)}, u32[]{:S(2)}) copy-start(s32[32,1]{0,1:T(1,128)} %param.17) | copy-start | bytes 388
  50.7 15.4 %copy-start.12 = (s32[32,4]{0,1:T(4,128)S(1)}, s32[32,4]{0,1:T(4,128)}, u32[]{:S(2)}) copy-start(s32[32,4]{0,1:T(4,128)} %param.16) | copy-start | bytes 1540
  50.7 15.4 %copy-start.13 = (s32[32,4]{0,1:T(4,128)S(1)}, s32[32,4]{0,1:T(4,128)}, u32[]{:S(2)}) copy-start(s32[32,4]{0,1:T(4,128)} %param.15) | copy-start | bytes 1540
  50.7 15.6 %copy-start.16 = (s32[16]{0:T(128)S(1)}, s32[16]{0:T(128)}, u32[]{:S(2)}) copy-start(s32[16]{0:T(128)} %constant.162) | copy-start | bytes 196
  50.7 17.6 %copy-start.10 = (f32[16,4,1]{0,1,2:T(4,128)S(1)}, f32[16,4,1]{0,1,2:T(4,128)}, u32[]{:S(2)}) copy-start(f32[16,4,1]{0,1,2:T(4,128)} %constant.166) | copy-start | bytes 772
  74.4 1.2 %copy-start.5 = (f32[32,12,5,128]{3,0,2,1:T(8,128)S(1)}, f32[32,12,5,128]{3,0,2,1:T(8,128)}, u32[]{:S(2)}) copy-start(f32[32,12,5,128]{3,0,2,1:T(8,128)} %copy.103) | copy-start | bytes 2949124
  89.7 1.6 %copy-start.8 = (f32[4,4,16,1,1]{2,0,4,3,1:T(4,128)S(1)}, f32[4,4,16,1,1]{2,0,4,3,1:T(4,128)}, u32[]{:S(2)}) copy-start(f32[4,4,16,1,1]{2,0,4,3,1:T(4,128)} %constant.164) | copy-start | bytes 3076
  90.1 4.0 %copy-start.3 = (f32[32,16,5,128]{3,2,1,0:T(8,128)S(1)}, f32[32,16,5,128]{3,2,1,0:T(8,128)}, u32[]{:S(2)}) copy-start(f32[32,16,5,128]{3,2,1,0:T(8,128)} %copy-done.2) | copy-start | bytes 3932164
  91.3 2.8 %copy-start.1 = (f32[32,4,4,5,128]{4,0,3,2,1:T(8,128)S(1)}, f32[32,4,4,5,128]{4,0,3,2,1:T(8,128)}, u32[]{:S(2)}) copy-start(f32[32,4,4,5,128]{4,0,3,2,1:T(8,128)} %copy-done) | copy-start | bytes 3932164
  91.3 2.9 %copy-start.6 = (f32[32,16,1,128]{3,1,0,2:T(8,128)S(1)}, f32[32,16,1,128]{3,1,0,2:T(8,128)}, u32[]{:S(2)}) copy-start(f32[32,16,1,128]{3,1,0,2:T(8,128)} %convolution_bitcast_fusion.1) | copy-start | bytes 786436
  91.3 2.9 %copy-start.15 = (f32[16]{0:T(128)S(1)}, f32[16]{0:T(128)}, u32[]{:S(2)}) copy-start(f32[16]{0:T(128)} %constant.143) | copy-start | bytes 196
where the time goes:
time: 99.5 us; the launch traced here: 97.6 us
  local copies, waits for them, and re-layouts  34.8 us (35%)
  other arithmetic  27.5 us (28%)
  starting transfers between devices  24.4 us (25%)
  matrix products  10.3 us (10%)
    reduce_sum x1, other arithmetic, physics(): jnp.mean(jnp.exp(path_in - path_all) - jnp.exp(path_out - path_all), axis=2)  15.1 us
    ppermute x1, starting transfers between devices, extended(): lax.ppermute(first, axis, [(b, a) for a, b in up])  15 us
    gather x2, local copies, waits for them, and re-layouts, per_device(): jnp.take(rim_wide, jnp.asarray(boundary_edge_table().reshape(-1), jnp.int...  8.89 us
    another operation x1, other arithmetic, physics(): path_in = jnp.cumsum(depth, axis=1)  8.53 us
    concatenate x4, local copies, waits for them, and re-layouts, extended(): jnp.concatenate([jnp.pad(low, around), value, jnp.pad(high, around)], axi...  5.51 us
    ppermute x1, starting transfers between devices, extended(): lax.ppermute(last, axis, up)  4.82 us
    all_to_all x1, starting transfers between devices, per_device(): lax.all_to_all(surface.reshape(cur_count, capacity * 4), 'cur', split_axi...  4.63 us
    gather x3, local copies, waits for them, and re-layouts, per_device(): jnp.take(tendency_own, jnp.asarray(boundary_points(), jnp.int32), axis=1)  4.09 us
  transfers between devices with their start and end apart: 3, of which 0 were waited for; matrix products, arithmetic and copies ran while one was open for 35% of the time, Pallas kernels for 0%

commit v1 on v0

v1 whole, which is shorter than its diff:
```python
import functools
import math

import jax
import jax.numpy as jnp
import numpy as np
from jax import lax
from jax.experimental import pallas as pl
from jax.experimental.pallas import tpu as pltpu
from jax.sharding import PartitionSpec as P

MESH = pl.DeviceIdType.MESH
F32 = jnp.float32
BF16 = jnp.bfloat16
EDGES = ((0, 4, 8, 12), (12, 13, 14, 15), (15, 11, 7, 3), (3, 2, 1, 0))
RIM = (0, 1, 2, 3, 4, 7, 8, 11, 12, 13, 14, 15)
INNER = (5, 6, 9, 10)
SEND_ORDER = (0, 1, 3, 4, 2)
NE = 32
NV = 5
NL = 128


def gll_matrix():
    nodes = np.array([-1.0, -1.0 / np.sqrt(5.0), 1.0 / np.sqrt(5.0), 1.0])
    weights = np.array(
        [1.0 / np.prod([nodes[c] - nodes[o] for o in range(4) if o != c]) for c in range(4)]
    )
    matrix = np.zeros((4, 4))
    for r in range(4):
        for c in range(4):
            if r != c:
                matrix[r, c] = weights[c] / weights[r] / (nodes[r] - nodes[c])
        matrix[r, r] = -np.sum(matrix[r])
    return matrix


def weighted(terms):
    total = None
    for weight, value in terms:
        if abs(weight) < 1e-12:
            continue
        part = value * float(weight)
        total = part if total is None else total + part
    return total


def slab(p, v):
    return pl.ds((p * NV + v) * NL, NL)


def split(x):
    high = x.astype(BF16)
    low = (x - high.astype(F32)).astype(BF16)
    return high, low


def fold(x):
    rows = x.shape[0] // 8
    parts = [x[8 * i : 8 * i + 8] for i in range(rows)]
    while len(parts) > 1:
        parts = [parts[i] + parts[i + 1] for i in range(0, len(parts), 2)]
    return parts[0]


def kernel(
    nx,
    nz,
    state,
    nbr,
    nedge,
    owner,
    surface,
    kw,
    kt,
    out,
    own,
    left,
    right,
    inner,
    cols,
    wt,
    tran,
    st_part,
    sp_part,
    sq_part,
    shift,
    onehot,
    rhs,
    zbuf,
    xbuf,
    rim_send,
    rim_recv,
    z_send,
    z_recv,
    x_send,
    x_recv,
    copy_sem,
):
    blk = lax.axis_index("blk")
    cur = lax.axis_index("cur")
    n_blk = lax.axis_size("blk")
    n_cur = nx * nz
    n_dev = n_blk * n_cur
    me = blk * n_cur + cur
    my_x = cur // nz
    my_z = cur % nz

    def place(index):
        return (index // n_cur, index % n_cur)

    after = place(lax.rem(me + 1, n_dev))
    before = place(lax.rem(me + n_dev - 1, n_dev))

    def z_peer(j):
        return (blk, my_x * nz + lax.rem(my_z + j, nz))

    def x_peer(j):
        return (blk, lax.rem(my_x + j, nx) * nz + my_z)

    barrier = pltpu.get_barrier_semaphore()
    peers = [after, before] + [z_peer(j) for j in range(1, nz)] + [x_peer(j) for j in range(1, nx)]
    for peer in peers:
        pl.semaphore_signal(barrier, inc=1, device_id=peer, device_id_type=MESH)
    keep = pltpu.make_async_copy(surface, zbuf.at[my_z], copy_sem.at[0])
    keep.start()

    d_matrix = -0.5 * gll_matrix()

    def tend_rows(g, _):
        rows = pl.ds(pl.multiple_of(8 * g, 8), 8)
        wind_u = [state[rows, slab(p, 0)] for p in range(16)]
        wind_v = [state[rows, slab(p, 1)] for p in range(16)]
        for v in range(NV):
            q = [state[rows, slab(p, v)] for p in range(16)]
            for i in range(4):
                for j in range(4):
                    p = 4 * i + j
                    qx = weighted([(d_matrix[i, a], q[4 * a + j]) for a in range(4)])
                    qy = weighted([(d_matrix[j, b], q[4 * i + b]) for b in range(4)])
                    tend = wind_u[p] * qx + wind_v[p] * qy
                    if p in RIM:
                        own[v, RIM.index(p), rows, :] = tend
                    else:
                        inner[v, INNER.index(p), rows, :] = tend
        return 0

    lax.fori_loop(0, NE // 8, tend_rows, 0)

    quad = (1.0 / 6.0, 5.0 / 6.0, 5.0 / 6.0, 1.0 / 6.0)
    for c in range(4):
        points = [4 * i + j for i in range(4) for j in range(4) if 2 * (i // 2) + j // 2 == c]
        for r in range(3):
            value = weighted(
                [(quad[p // 4] * quad[p % 4], state[:, slab(p, 2 + r)]) for p in points]
            )
            if r > 0:
                value = jnp.maximum(value, 0.0) + jnp.log1p(jnp.exp(-jnp.abs(value)))
            cols[r, pl.ds(NE * c, NE), :] = value
    for r in range(2):
        turned = cols[r + 1].T
        high = turned.astype(BF16).astype(F32)
        wt[2 * r] = high
        wt[2 * r + 1] = turned - high

    pl.semaphore_wait(barrier, len(peers))
    rim_copies = {}
    for v in SEND_ORDER:
        for side, (dst, peer) in enumerate(((left, after), (right, before))):
            copy = pltpu.make_async_remote_copy(
                src_ref=own.at[v],
                dst_ref=dst.at[v],
                send_sem=rim_send.at[side, v],
                recv_sem=rim_recv.at[side, v],
                device_id=peer,
                device_id_type=MESH,
            )
            copy.start()
            rim_copies[side, v] = copy
    z_copies = []
    for j in range(1, nz):
        copy = pltpu.make_async_remote_copy(
            src_ref=surface,
            dst_ref=zbuf.at[my_z],
            send_sem=z_send.at[j - 1],
            recv_sem=z_recv.at[j - 1],
            device_id=z_peer(j),
            device_id_type=MESH,
        )
        copy.start()
        z_copies.append(copy)
    keep.wait()

    row_in_16 = lax.broadcasted_iota(jnp.int32, (128, NL), 0) % 16
    scale = -math.log2(math.e)

    def depth_group(group, _):
        rows = pl.ds(pl.multiple_of(16 * group, 16), 16)
        kw_f = kw[rows, :] * scale
        kt_f = kt[rows, :] * scale
        kw_h = kw_f.astype(BF16).astype(F32)
        kt_h = kt_f.astype(BF16).astype(F32)
        zero = jnp.zeros((32, NL), F32)
        k_stack = jnp.concatenate(
            [kw_h, kw_h, kw_f - kw_h, kt_h, kt_h, kt_f - kt_h, zero], axis=0
        )
        k_turned = k_stack.T.astype(BF16)
        w_h, w_l, t_h, t_l = (wt[i, rows, :] for i in range(4))
        w_stack = jnp.concatenate([w_h, w_l, w_h, t_h, t_l, t_h, zero], axis=0)
        for i in range(16):
            one = jnp.where(row_in_16 == i, w_stack, 0.0).astype(BF16)
            power = jnp.dot(k_turned, one, preferred_element_type=F32)
            passed = jnp.exp2(power)
            level = 16 * group + i
            tran[level] = passed
            st_part[pl.ds(pl.multiple_of(8 * level, 8), 8), :] = fold(passed)
        return 0

    lax.fori_loop(0, NL // 16, depth_group, 0)

    for copy in z_copies:
        copy.wait()
    x_copies = []
    keep_x = pltpu.make_async_copy(zbuf, xbuf.at[my_x], copy_sem.at[1])
    keep_x.start()
    for j in range(1, nx):
        copy = pltpu.make_async_remote_copy(
            src_ref=zbuf,
            dst_ref=xbuf.at[my_x],
            send_sem=x_send.at[j - 1],
            recv_sem=x_recv.at[j - 1],
            device_id=x_peer(j),
            device_id_type=MESH,
        )
        copy.start()
        x_copies.append(copy)

    def march(level, carry):
        down, up = carry
        back = NL - 1 - level
        down = down * tran[level]
        sp_part[pl.ds(pl.multiple_of(8 * level, 8), 8), :] = fold(down)
        sq_part[pl.ds(pl.multiple_of(8 * back, 8), 8), :] = fold(up)
        up = up * tran[back]
        return down, up

    ones = jnp.ones((NL, NL), F32)
    lax.fori_loop(0, NL, march, (ones, ones))

    def total(part):
        return sum(part[pl.ds(s, NL, stride=8), :] for s in range(8))

    sum_t, sum_p, sum_q = total(st_part), total(sp_part), total(sq_part)
    shift[0, pl.ds(0, 8), :] = jnp.full((8, NL), float(NL), F32)
    shift[0, pl.ds(8, NL), :] = sum_p
    shift[1, pl.ds(0, 8), :] = jnp.broadcast_to(sum_p[NL - 1 : NL], (8, NL))
    shift[1, pl.ds(8, NL), :] = sum_q
    inv = 1.0 / NL
    downward = ((shift[0, pl.ds(7, NL), :] - sum_p) * (64.0 * inv)).T
    upward = ((sum_q - shift[1, pl.ds(7, NL), :]) * (2.0 * inv)).T
    emitted = (8.0 - sum_t * (8.0 * inv)).T

    base = me * NE - NE
    elems = n_dev * NE
    local = nbr[...] - base
    local = jnp.where(local < 0, local + elems, local)
    local = jnp.where(local >= elems, local - elems, local)
    target = nedge[...] * 192 + local
    lane = lax.broadcasted_iota(jnp.int32, (NE, 768), 1)
    for k in range(4):
        want = target[:, k : k + 1]
        hit = (lane == want) | (lane == want + 96)
        onehot[pl.ds(NE * k, NE), :] = hit.astype(F32).astype(BF16)

    own_col = owner[...].astype(F32)
    sub = lax.broadcasted_iota(jnp.int32, (NE, NL), 0)
    lan = lax.broadcasted_iota(jnp.int32, (NE, NL), 1)
    wide = jnp.broadcast_to(own_col, (NE, NL))
    own_row = jnp.sum(jnp.where(sub == lan, wide, 0.0), axis=0, keepdims=True)
    earlier = (wide == own_row) & (lan < sub)
    rank = jnp.sum(jnp.where(earlier, 1.0, 0.0), axis=1, keepdims=True).astype(jnp.int32)

    keep_x.wait()
    for copy in x_copies:
        copy.wait()
    width = surface.shape[1]
    owner_wide = jnp.broadcast_to(owner[...], (NE, width))
    picked = jnp.zeros((NE, width), F32)
    for x in range(nx):
        for z in range(nz):
            row = jnp.broadcast_to(xbuf[x, z], (NE, width))
            picked = jnp.where(owner_wide == x * nz + z, row, picked)
    s_lane = lax.broadcasted_iota(jnp.int32, (NE, width), 1)
    first = (cur * (width // (4 * n_cur)) + rank) * 4
    heat = []
    for c in range(4):
        surf = jnp.sum(jnp.where(s_lane == first + c, picked, 0.0), axis=1, keepdims=True)
        part = slice(NE * c, NE * c + NE)
        heat.append(
            0.2
            * (
                downward[part]
                + surf * upward[part]
                - jnp.tanh(cols[0, pl.ds(NE * c, NE), :]) * emitted[part]
            )
        )

    count = [1 + sum(p in edge for edge in EDGES) for p in range(16)]
    for v in SEND_ORDER:
        rim_copies[0, v].wait()
        rim_copies[1, v].wait()
        for f in range(4):
            for m in range(4):
                b = RIM.index(EDGES[f][3 - m])
                lanes = pl.ds(NL * m, NL)
                for s, ref in enumerate((left, own, right)):
                    high, low = split(ref[v, b])
                    rhs[pl.ds(192 * f + 32 * s, 32), lanes] = high
                    rhs[pl.ds(192 * f + 96 + 32 * s, 32), lanes] = low
        got = jnp.dot(onehot[...], rhs[...], preferred_element_type=F32)
        for p in range(16):
            if p in RIM:
                tend = own[v, RIM.index(p)]
            else:
                tend = inner[v, INNER.index(p)]
            for k in range(4):
                if p in EDGES[k]:
                    m = EDGES[k].index(p)
                    tend = tend + got[NE * k : NE * k + NE, NL * m : NL * m + NL]
            value = state[:, slab(p, v)] + tend * (0.2 / count[p])
            if v == 2:
                value = value + heat[2 * (p // 8) + (p % 4) // 2]
            out[:, slab(p, v)] = value


def per_device(nx, nz, state, neighbour, neighbour_edge, owner, surface, k_water, k_tracer):
    width = surface.shape[1]
    vmem = pl.BlockSpec(memory_space=pltpu.VMEM)
    sem = pltpu.SemaphoreType.DMA
    return pl.pallas_call(
        functools.partial(kernel, nx, nz),
        out_shape=jax.ShapeDtypeStruct(state.shape, F32),
        in_specs=[vmem] * 7,
        out_specs=vmem,
        scratch_shapes=[
            pltpu.VMEM((NV, 12, NE, NL), F32),
            pltpu.VMEM((NV, 12, NE, NL), F32),
            pltpu.VMEM((NV, 12, NE, NL), F32),
            pltpu.VMEM((NV, 4, NE, NL), F32),
            pltpu.VMEM((3, NL, NL), F32),
            pltpu.VMEM((4, NL, NL), F32),
            pltpu.VMEM((NL, NL, NL), F32),
            pltpu.VMEM((8 * NL, NL), F32),
            pltpu.VMEM((8 * NL, NL), F32),
            pltpu.VMEM((8 * NL, NL), F32),
            pltpu.VMEM((2, NL + 8, NL), F32),
            pltpu.VMEM((NL, 768), BF16),
            pltpu.VMEM((768, 512), BF16),
            pltpu.VMEM((nz, 1, width), F32),
            pltpu.VMEM((nx, nz, 1, width), F32),
            sem((2, NV)),
            sem((2, NV)),
            sem((max(nz - 1, 1),)),
            sem((max(nz - 1, 1),)),
            sem((max(nx - 1, 1),)),
            sem((max(nx - 1, 1),)),
            sem((2,)),
        ],
        compiler_params=pltpu.CompilerParams(collective_id=0, has_side_effects=True),
        name="dynamics_physics",
    )(state, neighbour, neighbour_edge, owner, surface, k_water, k_tracer)


def solution(mesh):
    n_cur = mesh.shape["cur"]
    nx = 4 if n_cur % 4 == 0 and n_cur > 4 else 2
    nz = n_cur // nx
    both = P(("blk", "cur"), None)
    return jax.shard_map(
        functools.partial(per_device, nx, nz),
        mesh=mesh,
        in_specs=(both, both, both, both, both, P(), P()),
        out_specs=both,
        check_vma=False,
    )
```

time: 99.5 us -> 58.3 us (0.59)
  the two profiles are of different devices: /device:TPU:1 before, /device:TPU:32 now
where the time goes in v1:
time: 58.3 us; the launch traced here: 58.1 us
  Pallas kernels  51.5 us (88%)
  local copies, waits for them, and re-layouts  6.51 us (11%)
    pallas_call x1, Pallas kernels, per_device(): pl.pallas_call(functools.partial(kernel, nx, nz), out_shape=jax.ShapeDtyp...  51.5 us
    unnamed x4, local copies, waits for them, and re-layouts  6.51 us

profile of v1, /device:TPU:32, one launch (start us, length us, event | category | flops | bytes accessed | tf_op | source)
XLA Modules:
  0.0 58.1 jit_solution(17780329479767533460)
XLA Ops:
  0.0 1.4 %copy.8.nbr = s32[32,4]{1,0:T(8,128)} copy(s32[32,4]{0,1:T(4,128)} %param.8) | data formatting | bytes 1024 | tf_op args[1]
  1.4 1.4 %copy.9.nedge = s32[32,4]{1,0:T(8,128)} copy(s32[32,4]{0,1:T(4,128)} %param.9) | data formatting | bytes 1024 | tf_op args[2]
  2.7 1.3 %copy.10.owner = s32[32,1]{1,0:T(8,128)} copy(s32[32,1]{0,1:T(1,128)} %param.10) | data formatting | bytes 256 | tf_op args[3]
  4.1 51.5 %dynamics_physics.1 = f32[32,10240]{1,0:T(8,128)} custom-call(f32[32,10240]{1,0:T(8,128)} %state.1, s32[32,4]{1,0:T(8,128)} %copy.8.nbr, s32[32,4]{1,0:T(8,128)} %copy.9.nedge, s32[32,1]{1,0:T(8,128)} %copy.10.owner, f32[1,384]{1,0:T(1,128)} %surface.1, f32[128,128]{1,0:T(8,128)} %kw.1, f32[128,128]{1,0:T(8,128)} %kt.1), custom_call_target="tpu_custom_call" | custom-call | tf_op jit(solution)/shard_map/dynamics_physics/pallas_call | solution.py:340
  55.6 2.5 %copy.12 = f32[32,10240]{1,0:T(8,128)} copy(f32[32,10240]{1,0:T(8,128)} %dynamics_physics.1) | data formatting | bytes 2621440

commit v2 on v1

--- a/solution.py
+++ b/solution.py
@@ -127,25 +127,50 @@
 
     d_matrix = -0.5 * gll_matrix()
 
-    def tend_rows(g, _):
+    def tend_rows(v, g, _):
         rows = pl.ds(pl.multiple_of(8 * g, 8), 8)
-        wind_u = [state[rows, slab(p, 0)] for p in range(16)]
-        wind_v = [state[rows, slab(p, 1)] for p in range(16)]
-        for v in range(NV):
-            q = [state[rows, slab(p, v)] for p in range(16)]
-            for i in range(4):
-                for j in range(4):
-                    p = 4 * i + j
-                    qx = weighted([(d_matrix[i, a], q[4 * a + j]) for a in range(4)])
-                    qy = weighted([(d_matrix[j, b], q[4 * i + b]) for b in range(4)])
-                    tend = wind_u[p] * qx + wind_v[p] * qy
-                    if p in RIM:
-                        own[v, RIM.index(p), rows, :] = tend
-                    else:
-                        inner[v, INNER.index(p), rows, :] = tend
+        q = [state[rows, slab(p, v)] for p in range(16)]
+        for i in range(4):
+            for j in range(4):
+                p = 4 * i + j
+                qx = weighted([(d_matrix[i, a], q[4 * a + j]) for a in range(4)])
+                qy = weighted([(d_matrix[j, b], q[4 * i + b]) for b in range(4)])
+                tend = state[rows, slab(p, 0)] * qx + state[rows, slab(p, 1)] * qy
+                if p in RIM:
+                    own[v, RIM.index(p), rows, :] = tend
+                else:
+                    inner[v, INNER.index(p), rows, :] = tend
         return 0
 
-    lax.fori_loop(0, NE // 8, tend_rows, 0)
+    lax.fori_loop(0, NE // 8, functools.partial(tend_rows, SEND_ORDER[0]), 0)
+    pl.semaphore_wait(barrier, len(peers))
+    z_copies = []
+    for j in range(1, nz):
+        copy = pltpu.make_async_remote_copy(
+            src_ref=surface,
+            dst_ref=zbuf.at[my_z],
+            send_sem=z_send.at[j - 1],
+            recv_sem=z_recv.at[j - 1],
+            device_id=z_peer(j),
+            device_id_type=MESH,
+        )
+        copy.start()
+        z_copies.append(copy)
+    rim_copies = {}
+    for v in SEND_ORDER:
+        if v != SEND_ORDER[0]:
+            lax.fori_loop(0, NE // 8, functools.partial(tend_rows, v), 0)
+        for side, (dst, peer) in enumerate(((left, after), (right, before))):
+            copy = pltpu.make_async_remote_copy(
+                src_ref=own.at[v],
+                dst_ref=dst.at[v],
+                send_sem=rim_send.at[side, v],
+                recv_sem=rim_recv.at[side, v],
+                device_id=peer,
+                device_id_type=MESH,
+            )
+            copy.start()
+            rim_copies[side, v] = copy
 
     quad = (1.0 / 6.0, 5.0 / 6.0, 5.0 / 6.0, 1.0 / 6.0)
     for c in range(4):
@@ -163,32 +188,6 @@
         wt[2 * r] = high
         wt[2 * r + 1] = turned - high
 
-    pl.semaphore_wait(barrier, len(peers))
-    rim_copies = {}
-    for v in SEND_ORDER:
-        for side, (dst, peer) in enumerate(((left, after), (right, before))):
-            copy = pltpu.make_async_remote_copy(
-                src_ref=own.at[v],
-                dst_ref=dst.at[v],
-                send_sem=rim_send.at[side, v],
-                recv_sem=rim_recv.at[side, v],
-                device_id=peer,
-                device_id_type=MESH,
-            )
-            copy.start()
-            rim_copies[side, v] = copy
-    z_copies = []
-    for j in range(1, nz):
-        copy = pltpu.make_async_remote_copy(
-            src_ref=surface,
-            dst_ref=zbuf.at[my_z],
-            send_sem=z_send.at[j - 1],
-            recv_sem=z_recv.at[j - 1],
-            device_id=z_peer(j),
-            device_id_type=MESH,
-        )
-        copy.start()
-        z_copies.append(copy)
     keep.wait()
 
     row_in_16 = lax.broadcasted_iota(jnp.int32, (128, NL), 0) % 16
@@ -267,24 +266,28 @@
     local = jnp.where(local >= elems, local - elems, local)
     target = nedge[...] * 192 + local
     lane = lax.broadcasted_iota(jnp.int32, (NE, 768), 1)
+    sub = lax.broadcasted_iota(jnp.int32, (NE, NE), 0)
+    lan = lax.broadcasted_iota(jnp.int32, (NE, NE), 1)
+
+    def column(row):
+        return jnp.sum(jnp.where(sub == lan, row, 0.0), axis=1, keepdims=True)
+
     for k in range(4):
-        want = target[:, k : k + 1]
+        row = jnp.broadcast_to(target[k : k + 1, :].astype(F32), (NE, NE))
+        want = column(row).astype(jnp.int32)
         hit = (lane == want) | (lane == want + 96)
         onehot[pl.ds(NE * k, NE), :] = hit.astype(F32).astype(BF16)
 
-    own_col = owner[...].astype(F32)
-    sub = lax.broadcasted_iota(jnp.int32, (NE, NL), 0)
-    lan = lax.broadcasted_iota(jnp.int32, (NE, NL), 1)
-    wide = jnp.broadcast_to(own_col, (NE, NL))
-    own_row = jnp.sum(jnp.where(sub == lan, wide, 0.0), axis=0, keepdims=True)
-    earlier = (wide == own_row) & (lan < sub)
+    own_row = jnp.broadcast_to(owner[...].astype(F32), (NE, NE))
+    own_col = column(own_row)
+    earlier = (own_col == own_row) & (lan < sub)
     rank = jnp.sum(jnp.where(earlier, 1.0, 0.0), axis=1, keepdims=True).astype(jnp.int32)
 
     keep_x.wait()
     for copy in x_copies:
         copy.wait()
     width = surface.shape[1]
-    owner_wide = jnp.broadcast_to(owner[...], (NE, width))
+    owner_wide = jnp.broadcast_to(own_col.astype(jnp.int32), (NE, width))
     picked = jnp.zeros((NE, width), F32)
     for x in range(nx):
         for z in range(nz):
@@ -339,7 +342,7 @@
     sem = pltpu.SemaphoreType.DMA
     return pl.pallas_call(
         functools.partial(kernel, nx, nz),
-        out_shape=jax.ShapeDtypeStruct(state.shape, F32),
+        out_shape=pltpu.VMEM(state.shape, F32),
         in_specs=[vmem] * 7,
         out_specs=vmem,
         scratch_shapes=[
@@ -368,7 +371,7 @@
         ],
         compiler_params=pltpu.CompilerParams(collective_id=0, has_side_effects=True),
         name="dynamics_physics",
-    )(state, neighbour, neighbour_edge, owner, surface, k_water, k_tracer)
+    )(state, neighbour.T, neighbour_edge.T, owner.T, surface, k_water, k_tracer)
 
 
 def solution(mesh):

time: 58.3 us -> 48.1 us (0.83)
  the two profiles are of different devices: /device:TPU:32 before, /device:TPU:1 now
where the time goes in v2:
time: 48.1 us; the launch traced here: 48 us
  Pallas kernels  46.9 us (98%)
  local copies, waits for them, and re-layouts  1.06 us (2%)
    pallas_call x1, Pallas kernels, per_device(): pl.pallas_call(functools.partial(kernel, nx, nz), out_shape=pltpu.VMEM(st...  46.9 us
    unnamed x1, local copies, waits for them, and re-layouts  1.06 us

profile of v2, /device:TPU:1, one launch (start us, length us, event | category | flops | bytes accessed | tf_op | source)
XLA Modules:
  0.0 48.0 jit_solution(18165246829714370682)
XLA Ops:
  0.0 46.9 %dynamics_physics.1 = f32[32,10240]{1,0:T(8,128)S(1)} custom-call(f32[32,10240]{1,0:T(8,128)} %state.1, s32[4,32]{1,0:T(4,128)} %bitcast.3, s32[4,32]{1,0:T(4,128)} %bitcast.4, s32[1,32]{1,0:T(1,128)} %bitcast.5, f32[1,384]{1,0:T(1,128)} %surface.1, f32[128,128]{1,0:T(8,128)} %kw.1, f32[128,128]{1,0:T(8,128)} %kt.1), custom_call_target="tpu_custom_call" | custom-call | tf_op jit(solution)/shard_map/dynamics_physics/pallas_call | solution.py:343
  46.9 1.1 %copy.9 = f32[32,10240]{1,0:T(8,128)} copy(f32[32,10240]{1,0:T(8,128)S(1)} %dynamics_physics.1) | data formatting | bytes 2621440

commit v3 on v2

--- a/solution.py
+++ b/solution.py
@@ -66,6 +66,14 @@
 def kernel(
     nx,
     nz,
+    state_in,
+    nbr_in,
+    nedge_in,
+    owner_in,
+    surface_in,
+    kw_in,
+    kt_in,
+    out,
     state,
     nbr,
     nedge,
@@ -73,7 +81,6 @@
     surface,
     kw,
     kt,
-    out,
     own,
     left,
     right,
@@ -96,6 +103,11 @@
     x_send,
     x_recv,
     copy_sem,
+    load_sem,
+    z_near,
+    z_mid,
+    z_far,
+    x_near,
 ):
     blk = lax.axis_index("blk")
     cur = lax.axis_index("cur")
@@ -113,17 +125,33 @@
     before = place(lax.rem(me + n_dev - 1, n_dev))
 
     def z_peer(j):
-        return (blk, my_x * nz + lax.rem(my_z + j, nz))
+        return (blk, my_x * nz + lax.rem(my_z + j + nz, nz))
 
     def x_peer(j):
-        return (blk, lax.rem(my_x + j, nx) * nz + my_z)
+        return (blk, lax.rem(my_x + j + nx, nx) * nz + my_z)
+
+    def tell(sem, peer):
+        pl.semaphore_signal(sem, inc=1, device_id=peer, device_id_type=MESH)
 
     barrier = pltpu.get_barrier_semaphore()
-    peers = [after, before] + [z_peer(j) for j in range(1, nz)] + [x_peer(j) for j in range(1, nx)]
+    peers = [after, before, z_peer(1), z_peer(-1), x_peer(1), x_peer(-1)]
     for peer in peers:
-        pl.semaphore_signal(barrier, inc=1, device_id=peer, device_id_type=MESH)
-    keep = pltpu.make_async_copy(surface, zbuf.at[my_z], copy_sem.at[0])
-    keep.start()
+        tell(barrier, peer)
+    loads = []
+    pairs = (
+        (state_in, state),
+        (surface_in, surface),
+        (kw_in, kw),
+        (kt_in, kt),
+        (nbr_in, nbr),
+        (nedge_in, nedge),
+        (owner_in, owner),
+    )
+    for i, (src, dst) in enumerate(pairs):
+        load = pltpu.make_async_copy(src, dst, load_sem.at[i])
+        load.start()
+        loads.append(load)
+    loads[0].wait()
 
     d_matrix = -0.5 * gll_matrix()
 
@@ -142,24 +170,12 @@
                     inner[v, INNER.index(p), rows, :] = tend
         return 0
 
-    lax.fori_loop(0, NE // 8, functools.partial(tend_rows, SEND_ORDER[0]), 0)
-    pl.semaphore_wait(barrier, len(peers))
-    z_copies = []
-    for j in range(1, nz):
-        copy = pltpu.make_async_remote_copy(
-            src_ref=surface,
-            dst_ref=zbuf.at[my_z],
-            send_sem=z_send.at[j - 1],
-            recv_sem=z_recv.at[j - 1],
-            device_id=z_peer(j),
-            device_id_type=MESH,
-        )
-        copy.start()
-        z_copies.append(copy)
+    def tend_of(v):
+        lax.fori_loop(0, NE // 8, functools.partial(tend_rows, v), 0)
+
     rim_copies = {}
-    for v in SEND_ORDER:
-        if v != SEND_ORDER[0]:
-            lax.fori_loop(0, NE // 8, functools.partial(tend_rows, v), 0)
+
+    def send_rim(v):
         for side, (dst, peer) in enumerate(((left, after), (right, before))):
             copy = pltpu.make_async_remote_copy(
                 src_ref=own.at[v],
@@ -171,6 +187,25 @@
             )
             copy.start()
             rim_copies[side, v] = copy
+
+    tend_of(SEND_ORDER[0])
+    pl.semaphore_wait(barrier, len(peers))
+    tell(z_near, z_peer(1))
+    tell(z_near, z_peer(-1))
+    tell(x_near, x_peer(1))
+    tell(x_near, x_peer(-1))
+    send_rim(SEND_ORDER[0])
+    tend_of(SEND_ORDER[1])
+    send_rim(SEND_ORDER[1])
+    for load in loads[1:]:
+        load.wait()
+    keep = pltpu.make_async_copy(surface, zbuf.at[my_z], copy_sem.at[0])
+    keep.start()
+    pl.semaphore_wait(z_near, 2)
+    tell(z_mid, z_peer(2))
+    tell(z_mid, z_peer(-2))
+    for v in SEND_ORDER[2:]:
+        tend_of(v)
 
     quad = (1.0 / 6.0, 5.0 / 6.0, 5.0 / 6.0, 1.0 / 6.0)
     for c in range(4):
@@ -187,8 +222,6 @@
         high = turned.astype(BF16).astype(F32)
         wt[2 * r] = high
         wt[2 * r + 1] = turned - high
-
-    keep.wait()
 
     row_in_16 = lax.broadcasted_iota(jnp.int32, (128, NL), 0) % 16
     scale = -math.log2(math.e)
@@ -215,8 +248,42 @@
             st_part[pl.ds(pl.multiple_of(8 * level, 8), 8), :] = fold(passed)
         return 0
 
-    lax.fori_loop(0, NL // 16, depth_group, 0)
-
+    half = NL // 32
+    pl.semaphore_wait(z_mid, 2)
+    tell(z_far, z_peer(2))
+    tell(z_far, z_peer(-2))
+    lax.fori_loop(0, half, depth_group, 0)
+    pl.semaphore_wait(z_far, 2)
+    pl.semaphore_wait(x_near, 2)
+    z_copies = []
+    for j in range(1, nz):
+        copy = pltpu.make_async_remote_copy(
+            src_ref=surface,
+            dst_ref=zbuf.at[my_z],
+            send_sem=z_send.at[j - 1],
+            recv_sem=z_recv.at[j - 1],
+            device_id=z_peer(j),
+            device_id_type=MESH,
+        )
+        copy.start()
+        z_copies.append(copy)
+    for v in SEND_ORDER[2:]:
+        send_rim(v)
+    lax.fori_loop(half, 2 * half, depth_group, 0)
+
+    def march(level, carry):
+        down, up = carry
+        back = NL - 1 - level
+        down = down * tran[level]
+        sp_part[pl.ds(pl.multiple_of(8 * level, 8), 8), :] = fold(down)
+        sq_part[pl.ds(pl.multiple_of(8 * back, 8), 8), :] = fold(up)
+        up = up * tran[back]
+        return down, up
+
+    ones = jnp.ones((NL, NL), F32)
+    lax.fori_loop(0, NL, march, (ones, ones))
+
+    keep.wait()
     for copy in z_copies:
         copy.wait()
     x_copies = []
@@ -233,18 +300,6 @@
         )
         copy.start()
         x_copies.append(copy)
-
-    def march(level, carry):
-        down, up = carry
-        back = NL - 1 - level
-        down = down * tran[level]
-        sp_part[pl.ds(pl.multiple_of(8 * level, 8), 8), :] = fold(down)
-        sq_part[pl.ds(pl.multiple_of(8 * back, 8), 8), :] = fold(up)
-        up = up * tran[back]
-        return down, up
-
-    ones = jnp.ones((NL, NL), F32)
-    lax.fori_loop(0, NL, march, (ones, ones))
 
     def total(part):
         return sum(part[pl.ds(s, NL, stride=8), :] for s in range(8))
@@ -339,13 +394,16 @@
 def per_device(nx, nz, state, neighbour, neighbour_edge, owner, surface, k_water, k_tracer):
     width = surface.shape[1]
     vmem = pl.BlockSpec(memory_space=pltpu.VMEM)
+    anywhere = pl.BlockSpec(memory_space=pl.ANY)
+    args = (state, neighbour.T, neighbour_edge.T, owner.T, surface, k_water, k_tracer)
     sem = pltpu.SemaphoreType.DMA
     return pl.pallas_call(
         functools.partial(kernel, nx, nz),
         out_shape=pltpu.VMEM(state.shape, F32),
-        in_specs=[vmem] * 7,
+        in_specs=[anywhere] * 7,
         out_specs=vmem,
         scratch_shapes=[
+            *[pltpu.VMEM(arg.shape, arg.dtype) for arg in args],
             pltpu.VMEM((NV, 12, NE, NL), F32),
             pltpu.VMEM((NV, 12, NE, NL), F32),
             pltpu.VMEM((NV, 12, NE, NL), F32),
@@ -368,10 +426,12 @@
             sem((max(nx - 1, 1),)),
             sem((max(nx - 1, 1),)),
             sem((2,)),
+            sem((7,)),
+            *[pltpu.SemaphoreType.REGULAR] * 4,
         ],
         compiler_params=pltpu.CompilerParams(collective_id=0, has_side_effects=True),
         name="dynamics_physics",
-    )(state, neighbour.T, neighbour_edge.T, owner.T, surface, k_water, k_tracer)
+    )(*args)
 
 
 def solution(mesh):

time: 48.1 us -> 46.4 us (0.965)
  Pallas kernels: 46.9 us -> 45.1 us
    pallas_call x1, Pallas kernels: 46.9 us -> 45.1 us  [per_device(): pl.pallas_call(functools.partial(kernel, nx, nz), out_shape=pltpu.VMEM(st...]
where the time goes in v3:
time: 46.4 us; the launch traced here: 46.2 us
  Pallas kernels  45.1 us (97%)
  local copies, waits for them, and re-layouts  1.06 us (2%)
    pallas_call x1, Pallas kernels, per_device(): pl.pallas_call(functools.partial(kernel, nx, nz), out_shape=pltpu.VMEM(st...  45.1 us
    unnamed x1, local copies, waits for them, and re-layouts  1.06 us

profile of v3, /device:TPU:1, one launch (start us, length us, event | category | flops | bytes accessed | tf_op | source)
XLA Modules:
  0.0 46.2 jit_solution(9288042985754179894)
XLA Ops:
  0.0 45.1 %dynamics_physics.1 = f32[32,10240]{1,0:T(8,128)S(1)} custom-call(f32[32,10240]{1,0:T(8,128)} %state_in.1, s32[4,32]{1,0:T(4,128)} %bitcast.3, s32[4,32]{1,0:T(4,128)} %bitcast.4, s32[1,32]{1,0:T(1,128)} %bitcast.5, f32[1,384]{1,0:T(1,128)} %surface_in.1, f32[128,128]{1,0:T(8,128)} %kw_in.1, f32[128,128]{1,0:T(8,128)} %kt_in.1), custom_call_target="tpu_custom_call" | custom-call | tf_op jit(solution)/shard_map/dynamics_physics/pallas_call | solution.py:400
  45.1 1.1 %copy.9 = f32[32,10240]{1,0:T(8,128)} copy(f32[32,10240]{1,0:T(8,128)S(1)} %dynamics_physics.1) | data formatting | bytes 2621440

commit v4 on v3

--- a/solution.py
+++ b/solution.py
@@ -195,8 +195,6 @@
     tell(x_near, x_peer(1))
     tell(x_near, x_peer(-1))
     send_rim(SEND_ORDER[0])
-    tend_of(SEND_ORDER[1])
-    send_rim(SEND_ORDER[1])
     for load in loads[1:]:
         load.wait()
     keep = pltpu.make_async_copy(surface, zbuf.at[my_z], copy_sem.at[0])
@@ -204,7 +202,7 @@
     pl.semaphore_wait(z_near, 2)
     tell(z_mid, z_peer(2))
     tell(z_mid, z_peer(-2))
-    for v in SEND_ORDER[2:]:
+    for v in SEND_ORDER[1:]:
         tend_of(v)
 
     quad = (1.0 / 6.0, 5.0 / 6.0, 5.0 / 6.0, 1.0 / 6.0)
@@ -267,7 +265,7 @@
         )
         copy.start()
         z_copies.append(copy)
-    for v in SEND_ORDER[2:]:
+    for v in SEND_ORDER[1:]:
         send_rim(v)
     lax.fori_loop(half, 2 * half, depth_group, 0)
 
@@ -338,30 +336,32 @@
     earlier = (own_col == own_row) & (lan < sub)
     rank = jnp.sum(jnp.where(earlier, 1.0, 0.0), axis=1, keepdims=True).astype(jnp.int32)
 
-    keep_x.wait()
-    for copy in x_copies:
-        copy.wait()
-    width = surface.shape[1]
-    owner_wide = jnp.broadcast_to(own_col.astype(jnp.int32), (NE, width))
-    picked = jnp.zeros((NE, width), F32)
-    for x in range(nx):
-        for z in range(nz):
-            row = jnp.broadcast_to(xbuf[x, z], (NE, width))
-            picked = jnp.where(owner_wide == x * nz + z, row, picked)
-    s_lane = lax.broadcasted_iota(jnp.int32, (NE, width), 1)
-    first = (cur * (width // (4 * n_cur)) + rank) * 4
-    heat = []
-    for c in range(4):
-        surf = jnp.sum(jnp.where(s_lane == first + c, picked, 0.0), axis=1, keepdims=True)
-        part = slice(NE * c, NE * c + NE)
-        heat.append(
-            0.2
-            * (
-                downward[part]
-                + surf * upward[part]
-                - jnp.tanh(cols[0, pl.ds(NE * c, NE), :]) * emitted[part]
+    def heating():
+        keep_x.wait()
+        for copy in x_copies:
+            copy.wait()
+        width = surface.shape[1]
+        owner_wide = jnp.broadcast_to(own_col.astype(jnp.int32), (NE, width))
+        picked = jnp.zeros((NE, width), F32)
+        for x in range(nx):
+            for z in range(nz):
+                row = jnp.broadcast_to(xbuf[x, z], (NE, width))
+                picked = jnp.where(owner_wide == x * nz + z, row, picked)
+        s_lane = lax.broadcasted_iota(jnp.int32, (NE, width), 1)
+        first = (cur * (width // (4 * n_cur)) + rank) * 4
+        heat = []
+        for c in range(4):
+            surf = jnp.sum(jnp.where(s_lane == first + c, picked, 0.0), axis=1, keepdims=True)
+            part = slice(NE * c, NE * c + NE)
+            heat.append(
+                0.2
+                * (
+                    downward[part]
+                    + surf * upward[part]
+                    - jnp.tanh(cols[0, pl.ds(NE * c, NE), :]) * emitted[part]
+                )
             )
-        )
+        return heat
 
     count = [1 + sum(p in edge for edge in EDGES) for p in range(16)]
     for v in SEND_ORDER:
@@ -375,6 +375,8 @@
                     high, low = split(ref[v, b])
                     rhs[pl.ds(192 * f + 32 * s, 32), lanes] = high
                     rhs[pl.ds(192 * f + 96 + 32 * s, 32), lanes] = low
+        if v == 2:
+            heat = heating()
         got = jnp.dot(onehot[...], rhs[...], preferred_element_type=F32)
         for p in range(16):
             if p in RIM:

time: 46.4 us -> 46.2 us (level)
  no operation moved by 1% of the time
where the time goes in v4:
time: 46.2 us; the launch traced here: 46 us
  Pallas kernels  45 us (97%)
  local copies, waits for them, and re-layouts  1.06 us (2%)
    pallas_call x1, Pallas kernels, per_device(): pl.pallas_call(functools.partial(kernel, nx, nz), out_shape=pltpu.VMEM(st...  45 us
    unnamed x1, local copies, waits for them, and re-layouts  1.06 us

profile of v4, /device:TPU:1, one launch (start us, length us, event | category | flops | bytes accessed | tf_op | source)
XLA Modules:
  0.0 46.0 jit_solution(4583128208002829114)
XLA Ops:
  0.0 45.0 %dynamics_physics.1 = f32[32,10240]{1,0:T(8,128)S(1)} custom-call(f32[32,10240]{1,0:T(8,128)} %state_in.1, s32[4,32]{1,0:T(4,128)} %bitcast.3, s32[4,32]{1,0:T(4,128)} %bitcast.4, s32[1,32]{1,0:T(1,128)} %bitcast.5, f32[1,384]{1,0:T(1,128)} %surface_in.1, f32[128,128]{1,0:T(8,128)} %kw_in.1, f32[128,128]{1,0:T(8,128)} %kt_in.1), custom_call_target="tpu_custom_call" | custom-call | tf_op jit(solution)/shard_map/dynamics_physics/pallas_call | solution.py:402
  45.0 1.1 %copy.9 = f32[32,10240]{1,0:T(8,128)} copy(f32[32,10240]{1,0:T(8,128)S(1)} %dynamics_physics.1) | data formatting | bytes 2621440

commit v5 on v4

--- a/solution.py
+++ b/solution.py
@@ -16,6 +16,7 @@
 RIM = (0, 1, 2, 3, 4, 7, 8, 11, 12, 13, 14, 15)
 INNER = (5, 6, 9, 10)
 SEND_ORDER = (0, 1, 3, 4, 2)
+EARLY = 3
 NE = 32
 NV = 5
 NL = 128
@@ -103,6 +104,7 @@
     x_send,
     x_recv,
     copy_sem,
+    row_sem,
     load_sem,
     z_near,
     z_mid,
@@ -138,8 +140,13 @@
     for peer in peers:
         tell(barrier, peer)
     loads = []
+    rows_in = []
+    for g in range(NE // 8):
+        rows = pl.ds(8 * g, 8)
+        load = pltpu.make_async_copy(state_in.at[rows, :], state.at[rows, :], row_sem.at[g])
+        load.start()
+        rows_in.append(load)
     pairs = (
-        (state_in, state),
         (surface_in, surface),
         (kw_in, kw),
         (kt_in, kt),
@@ -151,7 +158,6 @@
         load = pltpu.make_async_copy(src, dst, load_sem.at[i])
         load.start()
         loads.append(load)
-    loads[0].wait()
 
     d_matrix = -0.5 * gll_matrix()
 
@@ -188,21 +194,26 @@
             copy.start()
             rim_copies[side, v] = copy
 
-    tend_of(SEND_ORDER[0])
+    for g in range(NE // 8):
+        rows_in[g].wait()
+        tend_rows(SEND_ORDER[0], g, 0)
     pl.semaphore_wait(barrier, len(peers))
     tell(z_near, z_peer(1))
     tell(z_near, z_peer(-1))
     tell(x_near, x_peer(1))
     tell(x_near, x_peer(-1))
     send_rim(SEND_ORDER[0])
-    for load in loads[1:]:
+    for v in SEND_ORDER[1:EARLY]:
+        tend_of(v)
+        send_rim(v)
+    for load in loads:
         load.wait()
     keep = pltpu.make_async_copy(surface, zbuf.at[my_z], copy_sem.at[0])
     keep.start()
     pl.semaphore_wait(z_near, 2)
     tell(z_mid, z_peer(2))
     tell(z_mid, z_peer(-2))
-    for v in SEND_ORDER[1:]:
+    for v in SEND_ORDER[EARLY:]:
         tend_of(v)
 
     quad = (1.0 / 6.0, 5.0 / 6.0, 5.0 / 6.0, 1.0 / 6.0)
@@ -265,7 +276,7 @@
         )
         copy.start()
         z_copies.append(copy)
-    for v in SEND_ORDER[1:]:
+    for v in SEND_ORDER[EARLY:]:
         send_rim(v)
     lax.fori_loop(half, 2 * half, depth_group, 0)
 
@@ -365,18 +376,20 @@
 
     count = [1 + sum(p in edge for edge in EDGES) for p in range(16)]
     for v in SEND_ORDER:
-        rim_copies[0, v].wait()
-        rim_copies[1, v].wait()
-        for f in range(4):
-            for m in range(4):
-                b = RIM.index(EDGES[f][3 - m])
-                lanes = pl.ds(NL * m, NL)
-                for s, ref in enumerate((left, own, right)):
-                    high, low = split(ref[v, b])
-                    rhs[pl.ds(192 * f + 32 * s, 32), lanes] = high
-                    rhs[pl.ds(192 * f + 96 + 32 * s, 32), lanes] = low
         if v == 2:
             heat = heating()
+        for step in range(2):
+            if step == 1:
+                rim_copies[0, v].wait()
+                rim_copies[1, v].wait()
+            for f in range(4):
+                for m in range(4):
+                    b = RIM.index(EDGES[f][3 - m])
+                    lanes = pl.ds(NL * m, NL)
+                    for s, ref in ((1, own),) if step == 0 else ((0, left), (2, right)):
+                        high, low = split(ref[v, b])
+                        rhs[pl.ds(192 * f + 32 * s, 32), lanes] = high
+                        rhs[pl.ds(192 * f + 96 + 32 * s, 32), lanes] = low
         got = jnp.dot(onehot[...], rhs[...], preferred_element_type=F32)
         for p in range(16):
             if p in RIM:
@@ -428,7 +441,8 @@
             sem((max(nx - 1, 1),)),
             sem((max(nx - 1, 1),)),
             sem((2,)),
-            sem((7,)),
+            sem((NE // 8,)),
+            sem((6,)),
             *[pltpu.SemaphoreType.REGULAR] * 4,
         ],
         compiler_params=pltpu.CompilerParams(collective_id=0, has_side_effects=True),

time: 46.2 us -> 44.7 us (0.968)
  Pallas kernels: 45 us -> 43.5 us
    pallas_call x1, Pallas kernels: 45 us -> 43.5 us  [per_device(): pl.pallas_call(functools.partial(kernel, nx, nz), out_shape=pltpu.VMEM(st...]
where the time goes in v5:
time: 44.7 us; the launch traced here: 44.6 us
  Pallas kernels  43.5 us (97%)
  local copies, waits for them, and re-layouts  1.06 us (2%)
    pallas_call x1, Pallas kernels, per_device(): pl.pallas_call(functools.partial(kernel, nx, nz), out_shape=pltpu.VMEM(st...  43.5 us
    unnamed x1, local copies, waits for them, and re-layouts  1.06 us

profile of v5, /device:TPU:1, one launch (start us, length us, event | category | flops | bytes accessed | tf_op | source)
XLA Modules:
  0.0 44.6 jit_solution(5836611455203531247)
XLA Ops:
  0.0 43.5 %dynamics_physics.1 = f32[32,10240]{1,0:T(8,128)S(1)} custom-call(f32[32,10240]{1,0:T(8,128)} %state_in.1, s32[4,32]{1,0:T(4,128)} %bitcast.3, s32[4,32]{1,0:T(4,128)} %bitcast.4, s32[1,32]{1,0:T(1,128)} %bitcast.5, f32[1,384]{1,0:T(1,128)} %surface_in.1, f32[128,128]{1,0:T(8,128)} %kw_in.1, f32[128,128]{1,0:T(8,128)} %kt_in.1), custom_call_target="tpu_custom_call" | custom-call | tf_op jit(solution)/shard_map/dynamics_physics/pallas_call | solution.py:415
  43.5 1.1 %copy.9 = f32[32,10240]{1,0:T(8,128)} copy(f32[32,10240]{1,0:T(8,128)S(1)} %dynamics_physics.1) | data formatting | bytes 2621440

commit v6 on v5

--- a/solution.py
+++ b/solution.py
@@ -203,13 +203,32 @@
     tell(x_near, x_peer(1))
     tell(x_near, x_peer(-1))
     send_rim(SEND_ORDER[0])
+    for load in loads:
+        load.wait()
+    keep = pltpu.make_async_copy(surface, xbuf.at[my_x], copy_sem.at[0])
+    keep.start()
+    x_copies = []
+
+    def send_x(j):
+        copy = pltpu.make_async_remote_copy(
+            src_ref=surface,
+            dst_ref=xbuf.at[my_x],
+            send_sem=x_send.at[j - 1],
+            recv_sem=x_recv.at[j - 1],
+            device_id=x_peer(j),
+            device_id_type=MESH,
+        )
+        copy.start()
+        x_copies.append(copy)
+
+    for j in sorted({1, nx - 1}):
+        send_x(j)
     for v in SEND_ORDER[1:EARLY]:
         tend_of(v)
         send_rim(v)
-    for load in loads:
-        load.wait()
-    keep = pltpu.make_async_copy(surface, zbuf.at[my_z], copy_sem.at[0])
-    keep.start()
+    pl.semaphore_wait(x_near, 2)
+    for j in range(2, nx - 1):
+        send_x(j)
     pl.semaphore_wait(z_near, 2)
     tell(z_mid, z_peer(2))
     tell(z_mid, z_peer(-2))
@@ -262,12 +281,22 @@
     tell(z_far, z_peer(2))
     tell(z_far, z_peer(-2))
     lax.fori_loop(0, half, depth_group, 0)
+    keep.wait()
+    for copy in x_copies:
+        copy.wait()
+    per = surface.shape[1] // n_cur
+
+    def window(z):
+        first = (my_x * nz + z) * per // NL * NL
+        return xbuf.at[:, :, pl.ds(pl.multiple_of(first, NL), NL)]
+
+    keep_z = pltpu.make_async_copy(window(my_z), zbuf.at[my_z], copy_sem.at[1])
+    keep_z.start()
     pl.semaphore_wait(z_far, 2)
-    pl.semaphore_wait(x_near, 2)
     z_copies = []
     for j in range(1, nz):
         copy = pltpu.make_async_remote_copy(
-            src_ref=surface,
+            src_ref=window(lax.rem(my_z + j, nz)),
             dst_ref=zbuf.at[my_z],
             send_sem=z_send.at[j - 1],
             recv_sem=z_recv.at[j - 1],
@@ -292,24 +321,6 @@
     ones = jnp.ones((NL, NL), F32)
     lax.fori_loop(0, NL, march, (ones, ones))
 
-    keep.wait()
-    for copy in z_copies:
-        copy.wait()
-    x_copies = []
-    keep_x = pltpu.make_async_copy(zbuf, xbuf.at[my_x], copy_sem.at[1])
-    keep_x.start()
-    for j in range(1, nx):
-        copy = pltpu.make_async_remote_copy(
-            src_ref=zbuf,
-            dst_ref=xbuf.at[my_x],
-            send_sem=x_send.at[j - 1],
-            recv_sem=x_recv.at[j - 1],
-            device_id=x_peer(j),
-            device_id_type=MESH,
-        )
-        copy.start()
-        x_copies.append(copy)
-
     def total(part):
         return sum(part[pl.ds(s, NL, stride=8), :] for s in range(8))
 
@@ -348,18 +359,17 @@
     rank = jnp.sum(jnp.where(earlier, 1.0, 0.0), axis=1, keepdims=True).astype(jnp.int32)
 
     def heating():
-        keep_x.wait()
-        for copy in x_copies:
+        keep_z.wait()
+        for copy in z_copies:
             copy.wait()
-        width = surface.shape[1]
-        owner_wide = jnp.broadcast_to(own_col.astype(jnp.int32), (NE, width))
-        picked = jnp.zeros((NE, width), F32)
+        owner_wide = jnp.broadcast_to(own_col.astype(jnp.int32), (NE, NL))
+        picked = jnp.zeros((NE, NL), F32)
         for x in range(nx):
             for z in range(nz):
-                row = jnp.broadcast_to(xbuf[x, z], (NE, width))
+                row = jnp.broadcast_to(zbuf[z, x], (NE, NL))
                 picked = jnp.where(owner_wide == x * nz + z, row, picked)
-        s_lane = lax.broadcasted_iota(jnp.int32, (NE, width), 1)
-        first = (cur * (width // (4 * n_cur)) + rank) * 4
+        s_lane = lax.broadcasted_iota(jnp.int32, (NE, NL), 1)
+        first = lax.rem(cur * per, NL) + rank * 4
         heat = []
         for c in range(4):
             surf = jnp.sum(jnp.where(s_lane == first + c, picked, 0.0), axis=1, keepdims=True)
@@ -432,8 +442,8 @@
             pltpu.VMEM((2, NL + 8, NL), F32),
             pltpu.VMEM((NL, 768), BF16),
             pltpu.VMEM((768, 512), BF16),
-            pltpu.VMEM((nz, 1, width), F32),
-            pltpu.VMEM((nx, nz, 1, width), F32),
+            pltpu.VMEM((nz, nx, 1, NL), F32),
+            pltpu.VMEM((nx, 1, width), F32),
             sem((2, NV)),
             sem((2, NV)),
             sem((max(nz - 1, 1),)),

time: 44.7 us -> 43 us (0.962)
  Pallas kernels: 43.5 us -> 41.7 us
    pallas_call x1, Pallas kernels: 43.5 us -> 41.7 us  [per_device(): pl.pallas_call(functools.partial(kernel, nx, nz), out_shape=pltpu.VMEM(st...]
where the time goes in v6:
time: 43 us; the launch traced here: 42.8 us
  Pallas kernels  41.7 us (97%)
  local copies, waits for them, and re-layouts  1.06 us (2%)
    pallas_call x1, Pallas kernels, per_device(): pl.pallas_call(functools.partial(kernel, nx, nz), out_shape=pltpu.VMEM(st...  41.7 us
    unnamed x1, local copies, waits for them, and re-layouts  1.06 us

profile of v6, /device:TPU:1, one launch (start us, length us, event | category | flops | bytes accessed | tf_op | source)
XLA Modules:
  0.0 42.8 jit_solution(13131276147147429763)
XLA Ops:
  0.0 41.7 %dynamics_physics.1 = f32[32,10240]{1,0:T(8,128)S(1)} custom-call(f32[32,10240]{1,0:T(8,128)} %state_in.1, s32[4,32]{1,0:T(4,128)} %bitcast.3, s32[4,32]{1,0:T(4,128)} %bitcast.4, s32[1,32]{1,0:T(1,128)} %bitcast.5, f32[1,384]{1,0:T(1,128)} %surface_in.1, f32[128,128]{1,0:T(8,128)} %kw_in.1, f32[128,128]{1,0:T(8,128)} %kt_in.1), custom_call_target="tpu_custom_call" | custom-call | tf_op jit(solution)/shard_map/dynamics_physics/pallas_call | solution.py:425
  41.7 1.1 %copy.9 = f32[32,10240]{1,0:T(8,128)} copy(f32[32,10240]{1,0:T(8,128)S(1)} %dynamics_physics.1) | data formatting | bytes 2621440

commit v7 on v6

--- a/solution.py
+++ b/solution.py
@@ -141,11 +141,14 @@
         tell(barrier, peer)
     loads = []
     rows_in = []
-    for g in range(NE // 8):
-        rows = pl.ds(8 * g, 8)
-        load = pltpu.make_async_copy(state_in.at[rows, :], state.at[rows, :], row_sem.at[g])
-        load.start()
-        rows_in.append(load)
+    for part, (start, size) in enumerate(((0, 2 * NL), (2 * NL, 3 * NL))):
+        for p in range(16):
+            lanes = pl.ds(p * NV * NL + start, size)
+            load = pltpu.make_async_copy(
+                state_in.at[:, lanes], state.at[:, lanes], row_sem.at[part, p]
+            )
+            load.start()
+            rows_in.append(load)
     pairs = (
         (surface_in, surface),
         (kw_in, kw),
@@ -194,16 +197,16 @@
             copy.start()
             rim_copies[side, v] = copy
 
-    for g in range(NE // 8):
-        rows_in[g].wait()
-        tend_rows(SEND_ORDER[0], g, 0)
+    for load in rows_in[:16]:
+        load.wait()
+    tend_of(SEND_ORDER[0])
     pl.semaphore_wait(barrier, len(peers))
     tell(z_near, z_peer(1))
     tell(z_near, z_peer(-1))
     tell(x_near, x_peer(1))
     tell(x_near, x_peer(-1))
     send_rim(SEND_ORDER[0])
-    for load in loads:
+    for load in loads + rows_in[16:]:
         load.wait()
     keep = pltpu.make_async_copy(surface, xbuf.at[my_x], copy_sem.at[0])
     keep.start()
@@ -392,12 +395,14 @@
             if step == 1:
                 rim_copies[0, v].wait()
                 rim_copies[1, v].wait()
-            for f in range(4):
-                for m in range(4):
-                    b = RIM.index(EDGES[f][3 - m])
-                    lanes = pl.ds(NL * m, NL)
-                    for s, ref in ((1, own),) if step == 0 else ((0, left), (2, right)):
-                        high, low = split(ref[v, b])
+            for b in range(12):
+                spots = [
+                    (f, m) for f in range(4) for m in range(4) if EDGES[f][3 - m] == RIM[b]
+                ]
+                for s, ref in ((1, own),) if step == 0 else ((0, left), (2, right)):
+                    high, low = split(ref[v, b])
+                    for f, m in spots:
+                        lanes = pl.ds(NL * m, NL)
                         rhs[pl.ds(192 * f + 32 * s, 32), lanes] = high
                         rhs[pl.ds(192 * f + 96 + 32 * s, 32), lanes] = low
         got = jnp.dot(onehot[...], rhs[...], preferred_element_type=F32)
@@ -451,7 +456,7 @@
             sem((max(nx - 1, 1),)),
             sem((max(nx - 1, 1),)),
             sem((2,)),
-            sem((NE // 8,)),
+            sem((2, 16)),
             sem((6,)),
             *[pltpu.SemaphoreType.REGULAR] * 4,
         ],

time: 43 us -> 43 us (level)
  no operation moved by 1% of the time
where the time goes in v7:
time: 43 us; the launch traced here: 42.8 us
  Pallas kernels  41.8 us (97%)
  local copies, waits for them, and re-layouts  1.06 us (2%)
    pallas_call x1, Pallas kernels, per_device(): pl.pallas_call(functools.partial(kernel, nx, nz), out_shape=pltpu.VMEM(st...  41.8 us
    unnamed x1, local copies, waits for them, and re-layouts  1.06 us

profile of v7, /device:TPU:1, one launch (start us, length us, event | category | flops | bytes accessed | tf_op | source)
XLA Modules:
  0.0 42.8 jit_solution(8156168756031436135)
XLA Ops:
  0.0 41.8 %dynamics_physics.1 = f32[32,10240]{1,0:T(8,128)S(1)} custom-call(f32[32,10240]{1,0:T(8,128)} %state_in.1, s32[4,32]{1,0:T(4,128)} %bitcast.3, s32[4,32]{1,0:T(4,128)} %bitcast.4, s32[1,32]{1,0:T(1,128)} %bitcast.5, f32[1,384]{1,0:T(1,128)} %surface_in.1, f32[128,128]{1,0:T(8,128)} %kw_in.1, f32[128,128]{1,0:T(8,128)} %kt_in.1), custom_call_target="tpu_custom_call" | custom-call | tf_op jit(solution)/shard_map/dynamics_physics/pallas_call | solution.py:430
  41.8 1.1 %copy.9 = f32[32,10240]{1,0:T(8,128)} copy(f32[32,10240]{1,0:T(8,128)S(1)} %dynamics_physics.1) | data formatting | bytes 2621440
